TPU v7x, 32 devices: a whole 2x2x4 slice. The times are simulated.
32 devices in a mesh: band: 8 (over z, x), coef: 4 (over y, core).
Axes of the slice: x: 2, y: 2, z: 4, core: 2. Of those that a mesh axis runs over, the one named last changes fastest.
Arguments:
- coeffs: float32 [1024, 262144], P('band', 'coef'), may hold values from -320 to 320
- ref_block: float32 [1024, 262144], P('band', 'coef'), may hold values from -0.01171875 to 0.01171875
- index_map: int32 [262144], P('coef'), may hold values from 0 to 65535, as said below
- band_group: int32 [1024], P('band'), may hold values from 0 to 15
Outputs:
- ortho: float32 [1024, 262144], P('band', 'coef')
- band_residual: float32 [1024], P('band')
- group_residual: float32 [16], replicated
Inputs may be any that keep to these rules, and one draw needn't show every extreme that they name: Within each aligned slab of 65536 coefficients, index_map holds every number of 0 to 65535 once.
All inputs are finite; a program needn't handle non-finite values.
Results may differ from a plain program's by a relative error of at most 0.000098.
Values sent between devices are 32-bit elements; how exact they have to be, the bound alone decides.
A program may use at most 384 MiB of HBM per device.

v0:
```python
import jax
import jax.numpy as jnp
from jax import lax
from jax.sharding import PartitionSpec as P

NB = 1024
NGROUPS = 16


def local(coeffs, ref_block, index_map, band_group):
    columns = lax.all_to_all(coeffs, "band", split_axis=1, concat_axis=0, tiled=True)
    partial_value = jnp.dot(
        columns, columns.T, precision=lax.Precision.HIGHEST, preferred_element_type=jnp.float32
    )
    margin = lax.psum(partial_value, ("band", "coef"))
    factor = jnp.linalg.cholesky(margin)
    ortho_cols = lax.linalg.triangular_solve(factor, columns, left_side=True, lower=True)
    ortho = lax.all_to_all(ortho_cols, "band", split_axis=0, concat_axis=1, tiled=True)
    aligned = jnp.take(ortho, index_map, axis=1)
    squares = jnp.sum((aligned - ref_block) ** 2, axis=1)
    group_range = jnp.arange(NGROUPS, dtype=jnp.int32)
    totals = lax.psum(squares, "coef")
    band_residual = jnp.sqrt(totals + 1e-06)
    onehot = (band_group[:, None] == group_range[None, :]).astype(jnp.float32)
    terms = jnp.dot(
        band_residual, onehot, precision=lax.Precision.HIGHEST, preferred_element_type=jnp.float32
    )
    group_residual = lax.psum(terms, "band") * (NGROUPS / NB)
    return (ortho, band_residual, group_residual)


def solution(mesh):
    return jax.shard_map(
        local,
        mesh=mesh,
        in_specs=(P("band", "coef"), P("band", "coef"), P("coef"), P("band")),
        out_specs=(P("band", "coef"), P("band"), P()),
        check_vma=False,
    )
```

profile of v0, /device:TPU:0, one launch (start us, length us, event | category | flops | bytes accessed | tf_op | source)
XLA Modules:
  0.0 2639.5 jit_solution(11342121475017291769)
XLA Ops:
  7.2 33.4 %copy.17 = f32[128,65536]{0,1:T(8,128)} copy(f32[128,65536]{1,0:T(8,128)} %param.4) | data formatting | bytes 67108864 | tf_op args[0]
  40.6 31.1 %copy.18 = f32[128,8,8192]{2,0,1:T(8,128)} copy(f32[128,8,8192]{0,2,1:T(8,128)} %bitcast.156) | data formatting | bytes 67108864 | tf_op jit(solution)/shard_map/all_to_all | solution.py:11
  71.7 735.1 %all_to_all.38 = f32[128,8,8192]{2,0,1:T(8,128)} all-to-all(f32[128,8,8192]{2,0,1:T(8,128)} %copy.18), channel_id=1, replica_groups=mesh['band'=8,'coef'=4] {'band'}, dimensions={1} | all-to-all | bytes 67108864 | tf_op jit(solution)/shard_map/all_to_all | solution.py:11
  806.8 117.0 %fusion.74 = f32[1024,1024]{0,1:T(8,128)} fusion(f32[1024,8192]{1,0:T(8,128)} %bitcast.157), kind=kOutput, calls=%fused_computation.177 | convolution fusion | flops 103079215104 | bytes 37748736 | tf_op jit(solution)/shard_map/dot_general | solution.py:12
  923.9 141.6 %all-reduce.3.cloned.1.call-done = f32[1024,1024]{0,1:T(8,128)} async-done(((f32[1024,1024]{0,1:T(8,128)}), f32[1024,1024]{0,1:T(8,128)}) %all-reduce.3.cloned.1.call-update) | async-done | bytes 4194320 | tf_op jit(solution)/shard_map/psum | solution.py:15
  1077.8 11.7 cholesky.223
  1089.5 9.8 custom-call.62
  1105.8 11.9 cholesky.244
  1131.4 11.7 cholesky.468
  1157.7 11.9 cholesky.487
  1184.1 11.7 cholesky.506
  1197.1 10.2 custom-call.66
  1210.7 11.7 cholesky.526
  1236.5 11.9 cholesky.546
  1262.1 11.7 cholesky.564
  1285.6 23.2 while.1
  1308.8 78.8 %custom-call.69 = f32[8,128,128]{1,2,0:T(8,128)S(1)} custom-call(f32[8,128,128]{2,1,0:T(8,128)S(1)} %get-tuple-element.10), custom_call_target="InvertDiagBlocksLowerTriangular" | custom-call | tf_op jit(solution)/shard_map/triangular_solve | solution.py:17
  1387.6 12.6 constant_dynamic-update-slice_fusion.17
  1431.7 12.2 fusion.16
  1443.9 13.9 constant_dynamic-update-slice_fusion.14
  1457.7 14.0 fusion.19
  1471.8 12.5 constant_dynamic-update-slice_fusion.13
  1484.3 17.1 convolution_subtract_fusion.2
  1508.1 19.2 convolution_subtract_fusion.4
  1533.2 23.5 convolution_subtract_fusion.3
  1571.7 33.4 %copy.22 = f32[128,65536]{0,1:T(8,128)} copy(f32[128,65536]{1,0:T(8,128)} %param.5) | data formatting | bytes 67108864 | tf_op args[1]
  1605.3 687.3 %all-to-all-done.1 = f32[8,128,8192]{2,1,0:T(8,128)} async-done(((f32[8,128,8192]{2,1,0:T(8,128)}), f32[8,128,8192]{2,1,0:T(8,128)}, u32[]{:S(2)}, u32[]{:S(2)}) %all-to-all-start.1) | async-done | bytes 33554464 | tf_op jit(solution)/shard_map/all_to_all | solution.py:18
  2292.6 31.0 %copy.21 = f32[128,8,8192]{0,2,1:T(8,128)} copy(f32[128,8,8192]{2,0,1:T(8,128)} %bitcast.35) | data formatting | bytes 67108864 | tf_op jit(solution)/shard_map/all_to_all | solution.py:18
  2323.6 228.0 %gather_fusion = f32[65536,128]{1,0:T(8,128)} fusion(f32[128,65536]{0,1:T(8,128)} %bitcast.154, s32[65536]{0:T(1024)S(1)} %fusion.45), kind=kCustom, calls=%fused_computation | custom fusion | bytes 67371008 | tf_op jit(solution)/shard_map/jit(_take)/gather | solution.py:19
  2551.6 20.7 fusion.1
  2578.2 33.5 %copy.23 = f32[128,65536]{1,0:T(8,128)} copy(f32[128,65536]{0,1:T(8,128)} %bitcast.155) | data formatting | bytes 67108864
  2611.6 20.3 psum.23
  (102 shorter events, 189.5 us)
Async XLA Ops:
  7.2 1058.3 %all-reduce.3.cloned.1.call-start = ((), (), s32[]{:S(2)}) async-start(), calls=%async_computation.2 | async-start | bytes 8388608 | tf_op jit(solution)/shard_map/psum | solution.py:15
  1075.7 2.0 copy-start.3
  1400.2 31.5 %copy-start = (f32[128,8192]{1,0:T(8,128)}, f32[128,8192]{1,0:T(8,128)S(1)}, u32[]{:S(2)}) copy-start(f32[128,8192]{1,0:T(8,128)S(1)} %get-tuple-element.79) | copy-start | bytes 12582916
  1415.3 16.4 copy-start.1
  1431.7 12.2 copy-start.2
  1564.6 728.0 %all-to-all-start.1 = ((f32[8,128,8192]{2,1,0:T(8,128)}), f32[8,128,8192]{2,1,0:T(8,128)}, u32[]{:S(2)}, u32[]{:S(2)}) async-start(f32[8,128,8192]{2,1,0:T(8,128)} %bitcast.166), calls=%async_computation.1 | async-start | bytes 67108864 | tf_op jit(solution)/shard_map/all_to_all | solution.py:18
  1571.7 33.4 %copy-start.4 = (s32[65536]{0:T(1024)S(1)}, s32[65536]{0:T(1024)}, u32[]{:S(2)}) copy-start(s32[65536]{0:T(1024)} %param.6) | copy-start | bytes 786436
  2551.6 26.4 copy-start.5
  2578.0 33.7 %copy-start.6 = (f32[128]{0:T(128)}, f32[128]{0:T(128)S(1)}, u32[]{:S(2)}) copy-start(f32[128]{0:T(128)S(1)} %add_sqrt_fusion) | copy-start | bytes 1540
Sparse Core Ops, SparseCore 0:
  924.0 141.4 all-reduce.2
where the time goes:
time: 2650 us; the launch traced here: 2640 us
  waiting for transfers between devices  829 us (31%)
  blocking collectives  761 us (29%)
  local copies, waits for them, and re-layouts  424 us (16%)
  matrix products  317 us (12%)
  other arithmetic  282 us (11%)
    all_to_all x1, blocking collectives, local(): lax.all_to_all(coeffs, 'band', split_axis=1, concat_axis=0, tiled=True)  735 us
    all_to_all x1, waiting for transfers between devices, local(): lax.all_to_all(ortho_cols, 'band', split_axis=0, concat_axis=1, tiled=True)  687 us
    gather x1, local copies, waits for them, and re-layouts, local(): aligned = jnp.take(ortho, index_map, axis=1)  228 us
    another operation x15, matrix products, local(): lax.linalg.triangular_solve(factor, columns, left_side=True, lower=True)  177 us
    another operation x30, other arithmetic, local(): factor = jnp.linalg.cholesky(margin)  172 us
    psum x1, waiting for transfers between devices, local(): margin = lax.psum(partial_value, ('band', 'coef'))  142 us
    dot_general x1, matrix products, local(): jnp.dot(columns, columns.T, precision=lax.Precision.HIGHEST, preferred_el...  117 us
    unnamed x17, local copies, waits for them, and re-layouts  102 us
  transfers between devices with their start and end apart: 2, of which 2 were waited for; matrix products, arithmetic and copies ran while one was open for 1% of the time, Pallas kernels for 0%

commit v1 on v0

v1 whole, which is shorter than its diff:
```python
import jax
import jax.numpy as jnp
from jax import lax
from jax.sharding import PartitionSpec as P

NGROUPS = 16
BLOCK = 128
ROWS = 256


def high(a, b):
    return jnp.dot(a, b, precision=lax.Precision.HIGH, preferred_element_type=jnp.float32)


def highest(a, b):
    return jnp.dot(a, b, precision=lax.Precision.HIGHEST, preferred_element_type=jnp.float32)


def inverse_factor(margin):
    size = margin.shape[0]
    eye = jnp.eye(BLOCK, dtype=jnp.float32)
    rest = margin
    below = jnp.zeros((size, 0), jnp.float32)
    rows = []
    for start in range(0, size, BLOCK):
        corner = lax.linalg.cholesky(rest[:BLOCK, :BLOCK], symmetrize_input=False)
        inv = lax.linalg.triangular_solve(corner, eye, left_side=True, lower=True)
        row = jnp.concatenate([highest(inv, below[:BLOCK]), inv], axis=1) if start else inv
        rows.append(jnp.pad(row, ((0, 0), (0, size - row.shape[1]))))
        if start + BLOCK < size:
            panel = highest(rest[BLOCK:, :BLOCK], inv.T)
            change = highest(panel, row)
            below = jnp.pad(below[BLOCK:], ((0, 0), (0, BLOCK))) - change
            rest = rest[BLOCK:, BLOCK:] - highest(panel, panel.T)
    return jnp.concatenate(rows, axis=0)


def local(coeffs, ref_block, index_map, band_group):
    devices = lax.axis_size("band")
    bands, slab = coeffs.shape
    part = slab // devices
    total = bands * devices

    pieces = coeffs.reshape(bands, devices, part).transpose(1, 0, 2)
    columns = lax.all_to_all(pieces, "band", split_axis=0, concat_axis=0, tiled=True)
    columns = columns.reshape(total, part)

    _, inverse = lax.sort((index_map, jnp.arange(slab, dtype=jnp.int32)), num_keys=1)
    ref_own = jnp.take(ref_block, inverse, axis=1, unique_indices=True, mode="clip")

    tops = range(0, total, ROWS)
    strips = [high(columns[t : t + ROWS], columns[: t + ROWS].T) for t in tops]
    strips = lax.psum(jnp.concatenate(strips, axis=1), ("band", "coef"))
    lower, at = [], 0
    for t in tops:
        width = t + ROWS
        lower.append(jnp.pad(strips[:, at : at + width], ((0, 0), (0, total - width))))
        at += width
    lower = jnp.concatenate(lower, axis=0)
    low = jnp.tril(lower)
    margin = low + jnp.tril(lower, -1).T
    inv = inverse_factor(margin)

    ortho_cols = jnp.concatenate(
        [high(inv[t : t + ROWS, : t + ROWS], columns[: t + ROWS]) for t in tops], axis=0
    )
    back = lax.all_to_all(
        ortho_cols.reshape(devices, bands, part), "band", split_axis=0, concat_axis=0, tiled=True
    )
    ortho = back.transpose(1, 0, 2).reshape(bands, slab)
    squares = jnp.sum((ortho - ref_own) ** 2, axis=1)
    band_residual = jnp.sqrt(lax.psum(squares, "coef") + 1e-06)
    onehot = (band_group[:, None] == jnp.arange(NGROUPS, dtype=jnp.int32)[None, :]).astype(jnp.float32)
    terms = highest(band_residual, onehot)
    group_residual = lax.psum(terms, "band") * (NGROUPS / total)
    return (ortho, band_residual, group_residual)


def solution(mesh):
    return jax.shard_map(
        local,
        mesh=mesh,
        in_specs=(P("band", "coef"), P("band", "coef"), P("coef"), P("band")),
        out_specs=(P("band", "coef"), P("band"), P()),
        check_vma=False,
    )
```

time: 2650 us -> 2290 us (0.86)
  waiting for transfers between devices: 829 us -> 541 us
  matrix products: 317 us -> 165 us
  local copies, waits for them, and re-layouts: 424 us -> 519 us
    all_to_all x1, waiting for transfers between devices: 687 us -> 406 us  [local(): lax.all_to_all(ortho_cols.reshape(devices, bands, part), 'band', split_ax...]
    another operation x29 -> x8, matrix products: 200 us -> 2.14 us  [inverse_factor(): inv = lax.linalg.triangular_solve(corner, eye, left_side=True, lower=True)]
    slice x0 -> x24, local copies, waits for them, and re-layouts: none -> 133 us  [the longest x9 130 us: local(): strips = [high(columns[t:t + ROWS], columns[:t + ROWS].T) for t in tops]]
    another operation x33 -> x40, other arithmetic: 256 us -> 183 us  [the longest x24 99.4 us: inverse_factor(): corner = lax.linalg.cholesky(rest[:BLOCK, :BLOCK], symmetrize_input=False)]
    dot_general x2 -> x37, matrix products: 117 us -> 163 us  [the longest x8 134 us: high(): jnp.dot(a, b, precision=lax.Precision.HIGH, preferred_element_type=jnp.fl...]
    unnamed x17 -> x20, local copies, waits for them, and re-layouts: 102 us -> 68.8 us
    all_to_all x2 -> x1, local copies, waits for them, and re-layouts: 62.1 us -> 31.1 us  [local(): lax.all_to_all(pieces, 'band', split_axis=0, concat_axis=0, tiled=True)]
    gather x1 -> x2, local copies, waits for them, and re-layouts: 228 us -> 257 us  [local(): jnp.take(ref_block, inverse, axis=1, unique_indices=True, mode='clip')]
  transfers between devices with their start and end apart: 2 -> 2, of which waited for: 2 -> 2; matrix products, arithmetic and copies ran while one was open for 1% -> 14% of each run, Pallas kernels for 0% -> 0%
where the time goes in v1:
time: 2290 us; the launch traced here: 2270 us
  blocking collectives  761 us (33%)
  waiting for transfers between devices  541 us (24%)
  local copies, waits for them, and re-layouts  519 us (23%)
  other arithmetic  266 us (12%)
  matrix products  165 us (7%)
    all_to_all x1, blocking collectives, local(): lax.all_to_all(pieces, 'band', split_axis=0, concat_axis=0, tiled=True)  735 us
    all_to_all x1, waiting for transfers between devices, local(): lax.all_to_all(ortho_cols.reshape(devices, bands, part), 'band', split_ax...  406 us
    gather x2, local copies, waits for them, and re-layouts, local(): jnp.take(ref_block, inverse, axis=1, unique_indices=True, mode='clip')  257 us
    psum x1, waiting for transfers between devices, local(): strips = lax.psum(jnp.concatenate(strips, axis=1), ('band', 'coef'))  135 us
    dot_general x8, matrix products, high(): jnp.dot(a, b, precision=lax.Precision.HIGH, preferred_element_type=jnp.fl...  134 us
    slice x9, local copies, waits for them, and re-layouts, local(): strips = [high(columns[t:t + ROWS], columns[:t + ROWS].T) for t in tops]  130 us
    another operation x24, other arithmetic, inverse_factor(): corner = lax.linalg.cholesky(rest[:BLOCK, :BLOCK], symmetrize_input=False)  99.4 us
    another operation x16, other arithmetic, inverse_factor(): inv = lax.linalg.triangular_solve(corner, eye, left_side=True, lower=True)  83.9 us
  transfers between devices with their start and end apart: 2, of which 2 were waited for; matrix products, arithmetic and copies ran while one was open for 14% of the time, Pallas kernels for 0%

profile of v1, /device:TPU:0, one launch (start us, length us, event | category | flops | bytes accessed | tf_op | source)
XLA Modules:
  0.0 2275.0 jit_solution(11808679882351079061)
XLA Ops:
  7.2 33.4 %copy.37 = f32[128,65536]{0,1:T(8,128)} copy(f32[128,65536]{1,0:T(8,128)} %param.7) | data formatting | bytes 67108864 | tf_op args[0]
  40.6 735.1 %all_to_all.10 = f32[8,128,8192]{1,2,0:T(8,128)} all-to-all(f32[8,128,8192]{1,2,0:T(8,128)} %bitcast.125), channel_id=1, replica_groups=mesh['band'=8,'coef'=4] {'band'}, dimensions={0} | all-to-all | bytes 67108864 | tf_op jit(solution)/shard_map/all_to_all | solution.py:45
  775.7 23.5 %fusion.100 = (f32[2,128,8192]{1,2,0:T(8,128)}, f32[2,128,8192]{1,2,0:T(8,128)}, f32[2,128,8192]{1,2,0:T(8,128)}, f32[2,128,8192]{1,2,0:T(8,128)}) fusion(f32[8,128,8192]{1,2,0:T(8,128)} %all_to_all.10), kind=kLoop, calls=%fused_computation.177 | loop fusion | bytes 67108864 | tf_op jit(solution)/shard_map/slice | solution.py:52
  808.2 16.9 slice.228
  825.1 24.7 %copy.42 = f32[6,128,8192]{2,1,0:T(8,128)} copy(f32[6,128,8192]{1,2,0:T(8,128)} %slice.228) | data formatting | bytes 50331648 | tf_op jit(solution)/shard_map/slice | solution.py:52
  870.2 17.5 copy.40
  905.5 14.1 fusion.101
  919.5 22.3 fusion.103
  941.8 12.9 fusion.102
  954.8 31.1 %copy.44 = f32[8,128,8192]{2,1,0:T(8,128)} copy(f32[8,128,8192]{1,2,0:T(8,128)} %all_to_all.10) | data formatting | bytes 67108864 | tf_op jit(solution)/shard_map/all_to_all | solution.py:45
  985.9 19.7 fusion.104
  1007.3 135.5 %all-reduce.17.cloned.1.call-done = f32[256,2560]{0,1:T(8,128)} async-done(((f32[256,2560]{0,1:T(8,128)}), f32[256,2560]{0,1:T(8,128)}) %all-reduce.17.cloned.1.call-update) | async-done | bytes 2621456 | tf_op jit(solution)/shard_map/psum | solution.py:53
  1160.6 11.7 custom-call.20
  1191.2 11.9 custom-call.22
  1220.8 11.7 custom-call.24
  1250.5 11.7 custom-call.26
  1277.7 11.7 custom-call.28
  1302.4 11.9 custom-call.30
  1329.0 11.7 custom-call.32
  1365.8 11.7 custom-call.34
  1389.8 13.1 fusion.17
  1402.9 18.0 fusion.12
  1420.9 23.5 %fusion.6 = f32[256,8192]{1,0:T(8,128)} fusion(f32[1024,8192]{1,0:T(8,128)} %bitcast.119, f32[128,896]{1,0:T(8,128)S(1)} %pad_maximum_fusion.2, f32[128,128]{1,0:T(8,128)S(1)} %copy.56, f32[128,896]{1,0:T(8,128)S(1)} %fusion.105), kind=kOutput, calls=%fused_computation.35 | convolution fusion | flops 12885950464 | bytes 42926080 | tf_op jit(solution)/shard_map/dot_general | solution.py:12
  1444.4 23.6 %pad_maximum_fusion = f32[1024,8192]{1,0:T(8,128)} fusion(f32[256,8192]{1,0:T(8,128)} %fusion.6, f32[256,8192]{1,0:T(8,128)} %fusion.12, f32[256,8192]{1,0:T(8,128)} %fusion.17, f32[256,8192]{1,0:T(8,128)} %fusion.38), kind=kLoop, calls=%fused_computation.1 | loop fusion | flops 25165824 | bytes 67108864 | tf_op jit(solution)/shard_map/concatenate | solution.py:64
  1475.3 33.4 %copy.58 = f32[128,65536]{0,1:T(8,128)} copy(f32[128,65536]{1,0:T(8,128)} %param.8) | data formatting | bytes 67108864 | tf_op args[1]
  1508.8 25.5 %sort.15 = (s32[65536]{0:T(1024)}, s32[65536]{0:T(1024)S(1)}) sort(s32[65536]{0:T(1024)S(1)} %copy-done.5, s32[65536]{0:T(1024)S(1)} %iota.166), dimensions={0}, to_apply=%region_3.6 | sort | flops 1048576 | bytes 1048576 | tf_op jit(solution)/shard_map/sort | solution.py:48
  1534.3 226.1 %gather_fusion = f32[65536,128]{1,0:T(8,128)} fusion(f32[128,65536]{0,1:T(8,128)} %copy.58, s32[65536]{0:T(1024)S(1)} %broadcast_clamp_fusion), kind=kCustom, calls=%fused_computation | custom fusion | bytes 67371008 | tf_op jit(solution)/shard_map/jit(_take)/gather | solution.py:49
  1760.4 31.1 %copy.59 = f32[128,8,8192]{2,0,1:T(8,128)} copy(f32[128,8,8192]{0,2,1:T(8,128)} %bitcast.128) | data formatting | bytes 67108864 | tf_op jit(solution)/shard_map/jit(_take)/gather | solution.py:49
  1791.5 405.6 %all-to-all-done.1 = f32[8,128,8192]{2,1,0:T(8,128)} async-done(((f32[8,128,8192]{2,1,0:T(8,128)}), f32[8,128,8192]{2,1,0:T(8,128)}, u32[]{:S(2)}, u32[]{:S(2)}) %all-to-all-start.1) | async-done | bytes 33554464 | tf_op jit(solution)/shard_map/all_to_all | solution.py:67
  2197.1 20.9 fusion.1
  2223.8 20.4 psum.23
  2244.8 22.9 %copy.64 = f32[8,16,8,8192]{3,2,0,1:T(8,128)} copy(f32[8,16,8,8192]{3,2,1,0:T(8,128)} %bitcast.34) | data formatting | bytes 67108864 | tf_op jit(solution)/shard_map/reshape | solution.py:70
  (135 shorter events, 214.8 us)
Async XLA Ops:
  7.2 1135.6 %all-reduce.17.cloned.1.call-start = ((), (), s32[]{:S(2)}) async-start(), calls=%async_computation.2 | async-start | bytes 5242880 | tf_op jit(solution)/shard_map/psum | solution.py:53
  1005.5 139.5 %copy-start.6 = (pred[1024]{0:T(1024)(128)(4,1)S(1)}, pred[1024]{0:T(1024)(128)(4,1)}, u32[]{:S(2)}) copy-start(pred[1024]{0:T(1024)(128)(4,1)} %constant.30.clone.1) | copy-start | bytes 3076
  1158.7 1.9 copy-start
  1219.3 1.5 copy-start.1
  1302.4 23.7 %copy-start.2 = (f32[384,384]{1,0:T(8,128)}, f32[384,384]{1,0:T(8,128)S(1)}, u32[]{:S(2)}) copy-start(f32[384,384]{1,0:T(8,128)S(1)} %convolution_subtract_fusion.6) | copy-start | bytes 1769476
  1354.2 35.4 %copy-start.3 = (f32[128,512]{1,0:T(8,128)S(1)}, f32[128,512]{1,0:T(8,128)}, u32[]{:S(2)}) copy-start(f32[128,512]{1,0:T(8,128)} %pad_maximum_fusion.5) | copy-start | bytes 786436
  1354.2 35.6 %copy-start.4 = (f32[128,384]{1,0:T(8,128)S(1)}, f32[128,384]{1,0:T(8,128)}, u32[]{:S(2)}) copy-start(f32[128,384]{1,0:T(8,128)} %pad_maximum_fusion.6) | copy-start | bytes 589828
  1468.0 729.0 %all-to-all-start.1 = ((f32[8,128,8192]{2,1,0:T(8,128)}), f32[8,128,8192]{2,1,0:T(8,128)}, u32[]{:S(2)}, u32[]{:S(2)}) async-start(f32[8,128,8192]{2,1,0:T(8,128)} %bitcast.124), calls=%async_computation.1 | async-start | bytes 67108864 | tf_op jit(solution)/shard_map/all_to_all | solution.py:67
  1475.3 33.5 %copy-start.5 = (s32[65536]{0:T(1024)S(1)}, s32[65536]{0:T(1024)}, u32[]{:S(2)}) copy-start(s32[65536]{0:T(1024)} %param.9) | copy-start | bytes 786436
  1791.5 432.1 %copy-start.7 = (s32[128]{0:T(128)S(1)}, s32[128]{0:T(128)}, u32[]{:S(2)}) copy-start(s32[128]{0:T(128)} %param.10) | copy-start | bytes 1540
  2223.6 44.0 %copy-start.8 = (f32[128]{0:T(128)}, f32[128]{0:T(128)S(1)}, u32[]{:S(2)}) copy-start(f32[128]{0:T(128)S(1)} %add_sqrt_fusion) | copy-start | bytes 1540
Sparse Core Ops, SparseCore 0:
  1007.4 135.3 all-reduce.16
